TPU v7x, 128 devices: a whole 4x4x4 slice. The times are simulated.
128 devices in a mesh: slot: 32 (over y, z, core), hid: 4 (over x).
Axes of the slice: x: 4, y: 4, z: 4, core: 2. Of those that a mesh axis runs over, the one named last changes fastest.
Arguments:
- master: float32 [16, 3, 4, 393216], P(None, None, 'hid', 'slot'), may hold values from -0.125 to 0.125
- first_moment: float32 [16, 3, 4, 393216], P(None, None, 'hid', 'slot'), may hold values from -0.3 to 0.3
- second_moment: float32 [16, 3, 4, 393216], P(None, None, 'hid', 'slot'), may hold values from 0.0001 to 0.01
- slot_weights: bfloat16 [32, 3, 768, 2048], P('slot', None, 'hid'), may hold values from -0.125 to 0.125
- back_rows: bfloat16 [32, 1024, 2048], P('slot'), may hold values from -6 to 6
- readout: bfloat16 [32, 1024, 2048], P('slot'), may hold values from -0.25 to 0.25
- ref_logratio: float32 [32, 1024], P('slot'), may hold values from -9 to 0
- labels: int32 [32, 1024], P('slot'), may hold values 0 or 1
- place_cur: int32 [32], replicated, may hold values from 0 to 15, as said below
- place_next: int32 [32], replicated, may hold values from 0 to 15, as said below
- fwd_rows: bfloat16 [8192, 2048], P('slot', 'hid'), may hold values from -6 to 6
- routes: int32 [8192, 1], P('slot'), may hold values from 0 to 31; in each aligned block of 256 rows (0 to 255, 256 to 511, ...) at most 16 rows name the same one
Outputs:
- out_rows: bfloat16 [8192, 2048], P('slot', 'hid')
- new_master: float32 [16, 3, 4, 393216], P(None, None, 'hid', 'slot')
- new_first: float32 [16, 3, 4, 393216], P(None, None, 'hid', 'slot')
- new_second: float32 [16, 3, 4, 393216], P(None, None, 'hid', 'slot')
Inputs may be any that keep to these rules, and one draw needn't show every extreme that they name: `place_cur`: every expert 0 to 15 is held by at least one slot. `place_next`: every expert 0 to 15 is held by at least one slot. `routes`: the rows of one slot name any one slot at most 16 times, a bound that some block reaches.
All inputs are finite; a program needn't handle non-finite values. No bound on the sum of `labels` on one device may be relied on, other than what follows from the above.
Results may differ from a plain program's by a relative error of at most 0.008.
Values may be sent and summed in bfloat16 or wider, within the bound.
No kernel may reach another device: no remote copies, remote signals or barrier semaphores. Data moves between devices by JAX's collectives and lax.ppermute only.
A program may use at most 128 MiB of HBM per device.

v0:
```python
import jax
import jax.numpy as jnp
from jax import lax
from jax.sharding import PartitionSpec as P

beta_kto = 1.0
desired_weight = 1.0
undesired_weight = 1.33
learn_rate = 0.004
decay_first = 0.9
decay_second = 0.999
correct_first = 0.9999734386011124
correct_second = 0.09520785288629043
adam_eps = 1e-08
weight_decay = 0.1


def expert_pass(inputs, weights):
    across = (((1,), (1,)), ((), ()))
    gate_vals = lax.dot_general(inputs, weights[0], across, preferred_element_type=jnp.float32)
    up_vals = lax.dot_general(inputs, weights[1], across, preferred_element_type=jnp.float32)
    hidden = (gate_vals * jax.nn.sigmoid(gate_vals) * up_vals).astype(jnp.bfloat16)
    produced = jnp.dot(hidden, weights[2], preferred_element_type=jnp.float32)
    return (gate_vals, up_vals, hidden, produced)


def kto_slope(scores, labels, center):
    sigma_v = jax.nn.sigmoid(beta_kto * (scores - center))
    signed = jnp.where(labels == 1, -desired_weight, undesired_weight)
    return beta_kto * sigma_v * (1.0 - sigma_v) * signed


def expert_backward(inputs, direction, weights, slope, gate_vals, up_vals, hidden):
    d_expert = (slope[:, None] * direction.astype(jnp.float32)).astype(jnp.bfloat16)
    d_hidden = lax.dot_general(
        d_expert, weights[2], (((1,), (1,)), ((), ())), preferred_element_type=jnp.float32
    )
    sigma_g = jax.nn.sigmoid(gate_vals)
    d_gate = (d_hidden * up_vals * sigma_g * (1.0 + gate_vals * (1.0 - sigma_g))).astype(
        jnp.bfloat16
    )
    d_up = (d_hidden * gate_vals * sigma_g).astype(jnp.bfloat16)
    contract = (((0,), (0,)), ((), ()))
    grad_gate = lax.dot_general(d_gate, inputs, contract, preferred_element_type=jnp.float32)
    grad_up = lax.dot_general(d_up, inputs, contract, preferred_element_type=jnp.float32)
    grad_down = lax.dot_general(hidden, d_expert, contract, preferred_element_type=jnp.float32)
    return jnp.stack([grad_gate, grad_up, grad_down])


def adamw_update(master, first_moment, second_moment, summed):
    new_first = decay_first * first_moment + (1.0 - decay_first) * summed
    new_second = decay_second * second_moment + (1.0 - decay_second) * summed * summed
    update = new_first / correct_first / (jnp.sqrt(new_second / correct_second) + adam_eps)
    new_master = master - learn_rate * (update + weight_decay * master)
    return (new_master, new_first, new_second)


def shards(
    master,
    first_moment,
    second_moment,
    slot_weights,
    back_rows,
    readout,
    ref_logratio,
    labels,
    place_cur,
    place_next,
    fwd_rows,
    routes,
):
    slot_count = lax.axis_size("slot")
    experts_here = master.shape[0]
    weights = slot_weights[0]
    width = weights.shape[2]
    owned_units = master.shape[3] // width
    inputs = back_rows[0]
    direction = readout[0]
    gate_vals, up_vals, hidden, partial_value = expert_pass(inputs, weights)
    row_part = jnp.sum(partial_value * direction.astype(jnp.float32), axis=1)
    policy = lax.psum(row_part, "hid")
    scores = policy - ref_logratio[0]
    row_total = slot_count * inputs.shape[0]
    center = lax.psum(jnp.sum(scores), "slot") / row_total
    slope = kto_slope(scores, labels[0], center)
    grads = expert_backward(inputs, direction, weights, slope, gate_vals, up_vals, hidden)
    arrived = lax.all_to_all(
        grads[None].astype(jnp.bfloat16), "slot", split_axis=2, concat_axis=0, tiled=True
    ).astype(jnp.float32)
    arrived = arrived.reshape(slot_count, 3, 1, owned_units * width)
    owner_map = (place_cur[None, :] == jnp.arange(experts_here, dtype=jnp.int32)[:, None]).astype(
        jnp.float32
    )
    summed = jnp.einsum("es,sabc->eabc", owner_map, arrived, precision=lax.Precision.HIGHEST)
    new_master, new_first, new_second = adamw_update(master, first_moment, second_moment, summed)
    refreshed = new_master.astype(jnp.bfloat16)
    pick_map = (place_next[:, None] == jnp.arange(experts_here, dtype=jnp.int32)[None, :]).astype(
        jnp.bfloat16
    )
    picked = jnp.einsum(
        "se,eabc->sabc", pick_map, refreshed, preferred_element_type=jnp.float32
    ).astype(jnp.bfloat16)
    picked = picked.reshape(slot_count, 3, owned_units, width)
    resident = lax.all_to_all(picked, "slot", split_axis=0, concat_axis=2, tiled=True)[0]
    capacity = 2 * fwd_rows.shape[0] // slot_count
    quarter = fwd_rows.shape[1]
    target = routes[:, 0]
    target_map = (target[:, None] == jnp.arange(slot_count, dtype=jnp.int32)[None, :]).astype(
        jnp.int32
    )
    earlier = jnp.cumsum(target_map, axis=0) - target_map
    position = jnp.sum(earlier * target_map, axis=1)
    slot_place = target * capacity + position
    place_map = (
        slot_place[None, :] == jnp.arange(slot_count * capacity, dtype=jnp.int32)[:, None]
    ).astype(jnp.bfloat16)
    widened = lax.all_gather(fwd_rows, "hid", axis=1, tiled=True)
    buffer_rows = jnp.dot(place_map, widened, preferred_element_type=jnp.float32).astype(
        jnp.bfloat16
    )
    buffer_rows = buffer_rows.reshape(slot_count, capacity, widened.shape[1])
    arrived_rows = lax.all_to_all(
        buffer_rows, "slot", split_axis=0, concat_axis=0, tiled=True
    ).reshape(slot_count * capacity, widened.shape[1])
    fwd_partial = expert_pass(arrived_rows, resident)[3]
    totals = lax.psum(fwd_partial, "hid")
    shares = lax.dynamic_slice_in_dim(totals, lax.axis_index("hid") * quarter, quarter, 1)
    outgoing = shares.astype(jnp.bfloat16).reshape(slot_count, capacity, quarter)
    returned = lax.all_to_all(outgoing, "slot", split_axis=0, concat_axis=0, tiled=True).reshape(
        slot_count * capacity, quarter
    )
    out_rows = lax.dot_general(
        place_map, returned, (((0,), (0,)), ((), ())), preferred_element_type=jnp.float32
    ).astype(jnp.bfloat16)
    return (out_rows, new_master, new_first, new_second)


def solution(mesh):
    return jax.shard_map(
        shards,
        mesh=mesh,
        in_specs=(
            P(None, None, "hid", "slot"),
            P(None, None, "hid", "slot"),
            P(None, None, "hid", "slot"),
            P("slot", None, "hid", None),
            P("slot", None, None),
            P("slot", None, None),
            P("slot", None),
            P("slot", None),
            P(),
            P(),
            P("slot", "hid"),
            P("slot", None),
        ),
        out_specs=(
            P("slot", "hid"),
            P(None, None, "hid", "slot"),
            P(None, None, "hid", "slot"),
            P(None, None, "hid", "slot"),
        ),
        check_vma=False,
    )
```

profile of v0, /device:TPU:1, one launch (start us, length us, event | category | flops | bytes accessed | tf_op | source)
XLA Modules:
  0.0 364.6 jit_solution(15891182138285590733)
XLA Ops:
  7.2 4.1 %fusion.16 = f32[1024,192]{0,1:T(8,128)S(1)} fusion(bf16[1,1024,2048]{2,1,0:T(8,128)(2,1)} %param.16, bf16[1,3,192,2048]{3,2,1,0:T(8,128)(2,1)} %param.15), kind=kOutput, calls=%fused_computation.17 | convolution fusion | flops 805306368 | bytes 5767168 | tf_op jit(solution)/shard_map/dot_general | solution.py:20
  11.6 2.5 multiply_convert_fusion.2
  14.1 1.4 fusion.2
  15.5 9.3 %psum.21 = f32[1024]{0:T(1024)S(1)} all-reduce(f32[1024]{0:T(1024)S(1)} %fusion.2), channel_id=1, replica_groups=mesh['slot'=32,'hid'=4] {'hid'}, use_global_device_ids=true, to_apply=%region_4.5 | all-reduce | flops 1024 | bytes 8192 | tf_op jit(solution)/shard_map/psum | solution.py:81
  25.4 66.9 %psum.22 = f32[]{:T(128)} all-reduce(f32[]{:T(128)} %get-tuple-element.19), channel_id=1, replica_groups=mesh['slot'=32,'hid'=4] {'slot'}, use_global_device_ids=true, to_apply=%region_6.7 | all-reduce | flops 1 | bytes 8 | tf_op jit(solution)/shard_map/psum | solution.py:84
  93.0 4.0 %fusion.6 = f32[1024,192]{0,1:T(8,128)S(1)} fusion(bf16[1,1024,2048]{2,1,0:T(8,128)(2,1)} %param.17, f32[1024]{0:T(1024)S(1)} %fusion.71, bf16[1,3,192,2048]{3,2,1,0:T(8,128)(2,1)S(1)} %copy-done.13), kind=kOutput, calls=%fused_computation.9 | convolution fusion | flops 811597824 | bytes 5771264 | tf_op jit(solution)/shard_map/dot_general | solution.py:35
  101.7 2.0 copy.33
  103.8 45.2 %all_to_all.40 = bf16[1,3,192,2048]{3,1,0,2:T(4,128)(2,1)S(1)} all-to-all(bf16[1,3,192,2048]{3,1,0,2:T(4,128)(2,1)S(1)} %copy.33), channel_id=1, replica_groups=mesh['slot'=32,'hid'=4] {'slot'}, dimensions={2} | all-to-all | bytes 4718592 | tf_op jit(solution)/shard_map/all_to_all | solution.py:87
  148.9 1.7 copy.55
  150.7 4.5 %reshape.144 = bf16[32,3,12288]{2,0,1:T(8,128)(2,1)} reshape(bf16[32,1,3,6,2048]{4,3,0,2,1:T(8,128)(2,1)S(1)} %bitcast.131) | data formatting | bytes 4718592 | tf_op jit(solution)/shard_map/reshape.20
  155.2 11.4 %multiply_subtract_fusion = (f32[16,3,1,12288]{3,0,1,2:T(8,128)S(1)}, f32[16,3,1,12288]{3,0,1,2:T(8,128)}, f32[16,3,1,12288]{3,0,1,2:T(8,128)}) fusion(f32[16,3,1,12288]{3,2,1,0:T(1,128)} %param.12, f32[16,3,1,12288]{3,2,1,0:T(1,128)} %param.13, f32[16,3,1,12288]{3,2,1,0:T(1,128)} %param.14, bf16[32,3,12288]{2,0,1:T(8,128)(2,1)} %reshape.144, ...), kind=kOutput, calls=%fused_computation.36 | convolution fusion | flops 46596608 | bytes 16515200 | tf_op jit(solution)/shard_map/es,sabc->eabc/dot_general | solution.py:94
  166.5 1.4 copy-done
  167.9 2.2 convolution_convert_fusion
  170.2 5.0 %reshape.146 = bf16[32,3,6,2048]{3,2,0,1:T(8,128)(2,1)S(1)} reshape(bf16[32,3,12288]{2,0,1:T(8,128)(2,1)} %convolution_convert_fusion) | data formatting | bytes 4718592 | tf_op jit(solution)/shard_map/reshape | solution.py:103
  175.1 1.9 copy.38
  177.0 4.0 %all-to-all-start.2 = ((bf16[32,3,6,2048]{3,2,1,0:T(8,128)(2,1)}), bf16[32,3,6,2048]{3,2,1,0:T(8,128)(2,1)S(1)}, u32[]{:S(2)}, u32[]{:S(2)}) async-start(bf16[32,3,6,2048]{3,2,1,0:T(8,128)(2,1)} %copy.38), calls=%async_computation.2 | async-start | bytes 6291456 | tf_op jit(solution)/shard_map/all_to_all | solution.py:104
  182.8 21.8 %all-gather.2.cloned.1.call-done = bf16[256,2048]{1,0:T(8,128)(2,1)} async-done(((bf16[256,512]{1,0:T(8,128)(2,1)}), bf16[256,2048]{1,0:T(8,128)(2,1)}) %all-gather.2.cloned.1.call-update) | async-done | bytes 1048592 | tf_op jit(solution)/shard_map/all_gather | solution.py:117
  204.6 3.3 convolution_convert_fusion.1
  207.9 13.0 %all-to-all-done.2 = bf16[32,3,6,2048]{3,2,1,0:T(8,128)(2,1)S(1)} async-done(((bf16[32,3,6,2048]{3,2,1,0:T(8,128)(2,1)}), bf16[32,3,6,2048]{3,2,1,0:T(8,128)(2,1)S(1)}, u32[]{:S(2)}, u32[]{:S(2)}) %all-to-all-start.2) | async-done | bytes 2359328 | tf_op jit(solution)/shard_map/all_to_all | solution.py:104
  220.8 5.3 %all-to-all-start = ((bf16[32,16,2048]{2,1,0:T(8,128)(2,1)}), bf16[32,16,2048]{2,1,0:T(8,128)(2,1)}, u32[]{:S(2)}, u32[]{:S(2)}) async-start(bf16[32,16,2048]{2,1,0:T(8,128)(2,1)} %bitcast.132), calls=%async_computation | async-start | bytes 4194304 | tf_op jit(solution)/shard_map/all_to_all | solution.py:122
  226.1 1.8 fusion.79
  227.9 1.5 squeeze.38
  229.4 1.4 squeeze.39
  231.0 23.5 %all-to-all-done = bf16[32,16,2048]{2,1,0:T(8,128)(2,1)} async-done(((bf16[32,16,2048]{2,1,0:T(8,128)(2,1)}), bf16[32,16,2048]{2,1,0:T(8,128)(2,1)}, u32[]{:S(2)}, u32[]{:S(2)}) %all-to-all-start) | async-done | bytes 2097184 | tf_op jit(solution)/shard_map/all_to_all | solution.py:122
  254.6 2.4 fusion.80
  257.0 5.1 %fusion.43 = f32[512,2048]{1,0:T(8,128)} fusion(bf16[192,2048]{1,0:T(8,128)(2,1)S(1)} %squeeze.40, bf16[512,2048]{1,0:T(8,128)(2,1)} %bitcast.4, bf16[192,2048]{1,0:T(8,128)(2,1)S(1)} %squeeze.39, f32[512,192]{0,1:T(8,128)S(1)} %fusion.80), kind=kOutput, calls=%fused_computation.42 | convolution fusion | flops 805896192 | bytes 8257536 | tf_op jit(solution)/shard_map/dot_general | solution.py:23
  262.1 75.4 %all-reduce.1 = bf16[512,2048]{1,0:T(8,128)(2,1)} all-reduce(f32[512,2048]{1,0:T(8,128)} %fusion.43), channel_id=1, replica_groups=mesh['slot'=32,'hid'=4] {'hid'}, use_global_device_ids=true, to_apply=%region_7.8 | all-reduce | flops 1048576 | bytes 6291456 | tf_op jit(solution)/shard_map/psum | solution.py:126
  337.6 1.9 dynamic-slice_convert_fusion
  339.4 5.5 %all-to-all-start.3 = ((bf16[32,16,512]{2,1,0:T(8,128)(2,1)}), bf16[32,16,512]{2,1,0:T(8,128)(2,1)S(1)}, u32[]{:S(2)}, u32[]{:S(2)}) async-start(bf16[32,16,512]{2,1,0:T(8,128)(2,1)} %bitcast.26), calls=%async_computation.3 | async-start | bytes 1048576 | tf_op jit(solution)/shard_map/all_to_all | solution.py:129
  345.0 3.8 %copy.39 = f32[16,3,1,12288]{3,2,1,0:T(1,128)} copy(f32[16,3,1,12288]{3,0,1,2:T(8,128)S(1)} %copy-done.1) | data formatting | bytes 4718592
  348.8 3.8 %copy.40 = f32[16,3,1,12288]{3,2,1,0:T(1,128)} copy(f32[16,3,1,12288]{3,0,1,2:T(8,128)S(1)} %copy-done.4) | data formatting | bytes 4718592
  352.7 3.8 %copy.41 = f32[16,3,1,12288]{3,2,1,0:T(1,128)} copy(f32[16,3,1,12288]{3,0,1,2:T(8,128)S(1)} %copy-done.3) | data formatting | bytes 4718592
  (50 shorter events, 8.9 us)
Async XLA Ops:
  7.2 4.1 %copy-start.11 = (bf16[1,1024,2048]{2,1,0:T(8,128)(2,1)S(1)}, bf16[1,1024,2048]{2,1,0:T(8,128)(2,1)}, u32[]{:S(2)}) copy-start(bf16[1,1024,2048]{2,1,0:T(8,128)(2,1)} %param.16) | copy-start | bytes 12582916
  7.2 4.4 %copy-start.13 = (bf16[1,3,192,2048]{3,2,1,0:T(8,128)(2,1)S(1)}, bf16[1,3,192,2048]{3,2,1,0:T(8,128)(2,1)}, u32[]{:S(2)}) copy-start(bf16[1,3,192,2048]{3,2,1,0:T(8,128)(2,1)} %param.15) | copy-start | bytes 7077892
  11.6 2.5 copy-start.9
  14.1 10.7 %copy-start.6 = (f32[1,1024]{1,0:T(1,128)S(1)}, f32[1,1024]{1,0:T(1,128)}, u32[]{:S(2)}) copy-start(f32[1,1024]{1,0:T(1,128)} %param.18) | copy-start | bytes 12292
  14.1 78.2 %copy-start.7 = (s32[1,1024]{1,0:T(1,128)S(1)}, s32[1,1024]{1,0:T(1,128)}, u32[]{:S(2)}) copy-start(s32[1,1024]{1,0:T(1,128)} %param.19) | copy-start | bytes 12292
  93.0 4.0 %copy-start.10 = (bf16[1,1024,2048]{2,1,0:T(8,128)(2,1)S(1)}, bf16[1,1024,2048]{2,1,0:T(8,128)(2,1)}, u32[]{:S(2)}) copy-start(bf16[1,1024,2048]{2,1,0:T(8,128)(2,1)} %param.17) | copy-start | bytes 12582916
  96.9 2.2 copy-start.12
  99.1 1.1 copy-start.15
  150.6 4.5 %copy-start.14 = (s32[32]{0:T(128)S(1)}, s32[32]{0:T(128)}, u32[]{:S(2)}) copy-start(s32[32]{0:T(128)} %param.20) | copy-start | bytes 388
  155.2 12.8 %copy-start.8 = (s32[32]{0:T(128)S(1)}, s32[32]{0:T(128)}, u32[]{:S(2)}) copy-start(s32[32]{0:T(128)} %param.21) | copy-start | bytes 388
  166.5 1.4 copy-start
  177.0 4.8 %copy-start.5 = (s32[256,1]{0,1:T(1,128)S(1)}, s32[256,1]{0,1:T(1,128)}, u32[]{:S(2)}) copy-start(s32[256,1]{0,1:T(1,128)} %param.23) | copy-start | bytes 3076
  177.0 43.8 %all-to-all-start.2 = ((bf16[32,3,6,2048]{3,2,1,0:T(8,128)(2,1)}), bf16[32,3,6,2048]{3,2,1,0:T(8,128)(2,1)S(1)}, u32[]{:S(2)}, u32[]{:S(2)}) async-start(bf16[32,3,6,2048]{3,2,1,0:T(8,128)(2,1)} %copy.38), calls=%async_computation.2 | async-start | bytes 6291456 | tf_op jit(solution)/shard_map/all_to_all | solution.py:104
  181.1 23.5 %all-gather.2.cloned.1.call-start = ((), (), s32[]{:S(2)}) async-start(), calls=%async_computation.4 | async-start | bytes 1310720 | tf_op jit(solution)/shard_map/all_gather | solution.py:117
  220.8 33.7 %all-to-all-start = ((bf16[32,16,2048]{2,1,0:T(8,128)(2,1)}), bf16[32,16,2048]{2,1,0:T(8,128)(2,1)}, u32[]{:S(2)}, u32[]{:S(2)}) async-start(bf16[32,16,2048]{2,1,0:T(8,128)(2,1)} %bitcast.132), calls=%async_computation | async-start | bytes 4194304 | tf_op jit(solution)/shard_map/all_to_all | solution.py:122
  227.9 2.9 copy-start.2
  262.1 82.8 %copy-start.1 = (f32[16,3,1,12288]{3,0,1,2:T(8,128)S(1)}, f32[16,3,1,12288]{3,0,1,2:T(8,128)}, u32[]{:S(2)}) copy-start(f32[16,3,1,12288]{3,0,1,2:T(8,128)} %copy-done) | copy-start | bytes 7077892
  339.4 17.2 %all-to-all-start.3 = ((bf16[32,16,512]{2,1,0:T(8,128)(2,1)}), bf16[32,16,512]{2,1,0:T(8,128)(2,1)S(1)}, u32[]{:S(2)}, u32[]{:S(2)}) async-start(bf16[32,16,512]{2,1,0:T(8,128)(2,1)} %bitcast.26), calls=%async_computation.3 | async-start | bytes 1048576 | tf_op jit(solution)/shard_map/all_to_all | solution.py:129
  345.0 3.8 %copy-start.4 = (f32[16,3,1,12288]{3,0,1,2:T(8,128)S(1)}, f32[16,3,1,12288]{3,0,1,2:T(8,128)}, u32[]{:S(2)}) copy-start(f32[16,3,1,12288]{3,0,1,2:T(8,128)} %get-tuple-element.17) | copy-start | bytes 7077892
  348.8 3.8 %copy-start.3 = (f32[16,3,1,12288]{3,0,1,2:T(8,128)S(1)}, f32[16,3,1,12288]{3,0,1,2:T(8,128)}, u32[]{:S(2)}) copy-start(f32[16,3,1,12288]{3,0,1,2:T(8,128)} %get-tuple-element.18) | copy-start | bytes 7077892
Sparse Core Ops, SparseCore 0:
  183.5 21.0 all-gather.1
where the time goes:
time: 365 us
  blocking collectives  197 us (54%)
  waiting for transfers between devices  59.2 us (16%)
  matrix products  40.8 us (11%)
  local copies, waits for them, and re-layouts  36.4 us (10%)
  starting transfers between devices  14.9 us (4%)
  between operations  14.9 us (4%)
    psum x1, blocking collectives, shards(): totals = lax.psum(fwd_partial, 'hid')  75.4 us
    psum x1, blocking collectives, shards(): center = lax.psum(jnp.sum(scores), 'slot') / row_total  66.9 us
    all_to_all x1, blocking collectives, shards(): lax.all_to_all(grads[None].astype(jnp.bfloat16), 'slot', split_axis=2, co...  45.2 us
    all_to_all x1, waiting for transfers between devices, shards(): lax.all_to_all(buffer_rows, 'slot', split_axis=0, concat_axis=0, tiled=True)  23.5 us
    all_gather x1, waiting for transfers between devices, shards(): widened = lax.all_gather(fwd_rows, 'hid', axis=1, tiled=True)  21.8 us
    unnamed x35, local copies, waits for them, and re-layouts  14.4 us
    all_to_all x1, waiting for transfers between devices, shards(): lax.all_to_all(picked, 'slot', split_axis=0, concat_axis=2, tiled=True)[0]  13 us
    dot_general x1, matrix products, shards(): jnp.einsum('es,sabc->eabc', owner_map, arrived, precision=lax.Precision.H...  11.4 us
  transfers between devices with their start and end apart: 4, of which 4 were waited for; matrix products, arithmetic and copies ran while one was open for 6% of the time, Pallas kernels for 0%

commit v1 on v0

--- a/solution.py
+++ b/solution.py
@@ -123,7 +123,9 @@
         buffer_rows, "slot", split_axis=0, concat_axis=0, tiled=True
     ).reshape(slot_count * capacity, widened.shape[1])
     fwd_partial = expert_pass(arrived_rows, resident)[3]
-    totals = lax.psum(fwd_partial, "hid")
+    totals = fwd_partial
+    for hop in (1, 2):
+        totals = totals + lax.ppermute(totals, "hid", [(dev, dev ^ hop) for dev in range(4)])
     shares = lax.dynamic_slice_in_dim(totals, lax.axis_index("hid") * quarter, quarter, 1)
     outgoing = shares.astype(jnp.bfloat16).reshape(slot_count, capacity, quarter)
     returned = lax.all_to_all(outgoing, "slot", split_axis=0, concat_axis=0, tiled=True).reshape(

time: 365 us -> 488 us (1.34); the launches traced: 365 us -> 480 us
  waiting for transfers between devices: 59.2 us -> 243 us
  blocking collectives: 197 us -> 122 us
  other arithmetic: 1.62 us -> 9.72 us
    ppermute x0 -> x2, waiting for transfers between devices: none -> 183 us  [shards(): lax.ppermute(totals, 'hid', [(dev, dev ^ hop) for dev in range(4)])]
    psum x1 -> x0, blocking collectives: 75.4 us -> none  [shards(): totals = lax.psum(fwd_partial, 'hid')]
    add x0 -> x1, other arithmetic: none -> 4.92 us  [shards(): totals + lax.ppermute(totals, 'hid', [(dev, dev ^ hop) for dev in range(4)])]
    unnamed x35 -> x33, local copies, waits for them, and re-layouts: 14.4 us -> 13.9 us
  transfers between devices with their start and end apart: 4 -> 6, of which waited for: 4 -> 6; matrix products, arithmetic and copies ran while one was open for 6% -> 4% of each run, Pallas kernels for 0% -> 0%
where the time goes in v1:
time: 488 us; the launch traced here: 480 us
  waiting for transfers between devices  243 us (50%)
  blocking collectives  122 us (25%)
  matrix products  40.8 us (8%)
  local copies, waits for them, and re-layouts  34.1 us (7%)
  starting transfers between devices  16 us (3%)
  between operations  15.3 us (3%)
  other arithmetic  9.72 us (2%)
    ppermute x2, waiting for transfers between devices, shards(): lax.ppermute(totals, 'hid', [(dev, dev ^ hop) for dev in range(4)])  183 us
    psum x1, blocking collectives, shards(): center = lax.psum(jnp.sum(scores), 'slot') / row_total  66.9 us
    all_to_all x1, blocking collectives, shards(): lax.all_to_all(grads[None].astype(jnp.bfloat16), 'slot', split_axis=2, co...  45.4 us
    all_to_all x1, waiting for transfers between devices, shards(): lax.all_to_all(buffer_rows, 'slot', split_axis=0, concat_axis=0, tiled=True)  23.6 us
    all_gather x1, waiting for transfers between devices, shards(): widened = lax.all_gather(fwd_rows, 'hid', axis=1, tiled=True)  21.9 us
    unnamed x33, local copies, waits for them, and re-layouts  13.9 us
    all_to_all x1, waiting for transfers between devices, shards(): lax.all_to_all(picked, 'slot', split_axis=0, concat_axis=2, tiled=True)[0]  13 us
    dot_general x1, matrix products, shards(): jnp.einsum('es,sabc->eabc', owner_map, arrived, precision=lax.Precision.H...  11.4 us
  transfers between devices with their start and end apart: 6, of which 6 were waited for; matrix products, arithmetic and copies ran while one was open for 4% of the time, Pallas kernels for 0%

profile of v1, /device:TPU:1, one launch (start us, length us, event | category | flops | bytes accessed | tf_op | source)
XLA Modules:
  0.0 479.9 jit_solution(17588185481754723676)
XLA Ops:
  7.9 4.1 fusion.16
  12.3 2.5 multiply_convert_fusion.2
  16.2 9.3 %psum.14 = f32[1024]{0:T(1024)S(1)} all-reduce(f32[1024]{0:T(1024)S(1)} %fusion.2), channel_id=1, replica_groups=mesh['slot'=32,'hid'=4] {'hid'}, use_global_device_ids=true, to_apply=%region_4.5 | all-reduce | flops 1024 | bytes 8192 | tf_op jit(solution)/shard_map/psum | solution.py:81
  26.1 66.9 %psum.15 = f32[]{:T(128)} all-reduce(f32[]{:T(128)} %get-tuple-element.19), channel_id=1, replica_groups=mesh['slot'=32,'hid'=4] {'slot'}, use_global_device_ids=true, to_apply=%region_6.7 | all-reduce | flops 1 | bytes 8 | tf_op jit(solution)/shard_map/psum | solution.py:84
  93.6 3.4 fusion.35
  97.1 1.6 fusion.6
  101.9 2.0 copy.33
  103.9 45.4 %all_to_all.40 = bf16[1,3,192,2048]{3,1,0,2:T(4,128)(2,1)S(1)} all-to-all(bf16[1,3,192,2048]{3,1,0,2:T(4,128)(2,1)S(1)} %copy.33), channel_id=1, replica_groups=mesh['slot'=32,'hid'=4] {'slot'}, dimensions={2} | all-to-all | bytes 4718592 | tf_op jit(solution)/shard_map/all_to_all | solution.py:87
  149.3 1.7 copy.55
  151.0 4.5 reshape.144
  155.5 11.4 %multiply_subtract_fusion = (f32[16,3,1,12288]{3,0,1,2:T(8,128)S(1)}, f32[16,3,1,12288]{3,0,1,2:T(8,128)}, f32[16,3,1,12288]{3,0,1,2:T(8,128)}) fusion(f32[16,3,1,12288]{3,2,1,0:T(1,128)} %param.12, f32[16,3,1,12288]{3,2,1,0:T(1,128)} %param.13, f32[16,3,1,12288]{3,2,1,0:T(1,128)} %param.14, bf16[32,3,12288]{2,0,1:T(8,128)(2,1)} %reshape.144, ...), kind=kOutput, calls=%fused_computation.36 | convolution fusion | flops 46596608 | bytes 16515200 | tf_op jit(solution)/shard_map/es,sabc->eabc/dot_general | solution.py:94
  168.3 2.2 convolution_convert_fusion
  170.5 5.0 %reshape.146 = bf16[32,3,6,2048]{3,2,0,1:T(8,128)(2,1)S(1)} reshape(bf16[32,3,12288]{2,0,1:T(8,128)(2,1)} %convolution_convert_fusion) | data formatting | bytes 4718592 | tf_op jit(solution)/shard_map/reshape | solution.py:103
  175.5 1.9 copy.38
  177.4 4.0 all-to-all-start.2
  183.1 21.9 %all-gather.2.cloned.1.call-done = bf16[256,2048]{1,0:T(8,128)(2,1)} async-done(((bf16[256,512]{1,0:T(8,128)(2,1)}), bf16[256,2048]{1,0:T(8,128)(2,1)}) %all-gather.2.cloned.1.call-update) | async-done | bytes 1048592 | tf_op jit(solution)/shard_map/all_gather | solution.py:117
  205.0 3.3 convolution_convert_fusion.1
  208.3 13.0 %all-to-all-done.2 = bf16[32,3,6,2048]{3,2,1,0:T(8,128)(2,1)S(1)} async-done(((bf16[32,3,6,2048]{3,2,1,0:T(8,128)(2,1)}), bf16[32,3,6,2048]{3,2,1,0:T(8,128)(2,1)S(1)}, u32[]{:S(2)}, u32[]{:S(2)}) %all-to-all-start.2) | async-done | bytes 2359328 | tf_op jit(solution)/shard_map/all_to_all | solution.py:104
  221.2 5.3 %all-to-all-start = ((bf16[32,16,2048]{2,1,0:T(8,128)(2,1)}), bf16[32,16,2048]{2,1,0:T(8,128)(2,1)}, u32[]{:S(2)}, u32[]{:S(2)}) async-start(bf16[32,16,2048]{2,1,0:T(8,128)(2,1)} %bitcast.132), calls=%async_computation | async-start | bytes 4194304 | tf_op jit(solution)/shard_map/all_to_all | solution.py:122
  226.5 1.7 fusion.80
  228.2 1.5 squeeze.38
  231.4 23.6 %all-to-all-done = bf16[32,16,2048]{2,1,0:T(8,128)(2,1)} async-done(((bf16[32,16,2048]{2,1,0:T(8,128)(2,1)}), bf16[32,16,2048]{2,1,0:T(8,128)(2,1)}, u32[]{:S(2)}, u32[]{:S(2)}) %all-to-all-start) | async-done | bytes 2097184 | tf_op jit(solution)/shard_map/all_to_all | solution.py:122
  255.0 2.4 fusion.81
  257.4 5.1 %fusion.43 = f32[512,2048]{1,0:T(8,128)} fusion(bf16[192,2048]{1,0:T(8,128)(2,1)S(1)} %squeeze.40, bf16[512,2048]{1,0:T(8,128)(2,1)} %bitcast.4, bf16[192,2048]{1,0:T(8,128)(2,1)S(1)} %squeeze.39, f32[512,192]{0,1:T(8,128)S(1)} %fusion.81), kind=kOutput, calls=%fused_computation.42 | convolution fusion | flops 805896192 | bytes 8257536 | tf_op jit(solution)/shard_map/dot_general | solution.py:23
  262.6 91.5 %collective-permute-done = f32[512,2048]{1,0:T(8,128)S(1)} collective-permute-done((f32[512,2048]{1,0:T(8,128)}, f32[512,2048]{1,0:T(8,128)S(1)}, u32[]{:S(2)}, u32[]{:S(2)}) %collective-permute-start) | collective-permute-done | bytes 4194336 | tf_op jit(solution)/shard_map/ppermute | solution.py:128
  354.1 4.9 %add.58 = f32[512,2048]{1,0:T(8,128)} add(f32[512,2048]{1,0:T(8,128)} %fusion.43, f32[512,2048]{1,0:T(8,128)S(1)} %collective-permute-done) | non-fusion elementwise | flops 1048576 | bytes 12582912 | tf_op jit(solution)/shard_map/add | solution.py:128
  359.6 91.7 %collective-permute-done.1 = f32[512,2048]{1,0:T(8,128)} collective-permute-done((f32[512,2048]{1,0:T(8,128)}, f32[512,2048]{1,0:T(8,128)}, u32[]{:S(2)}, u32[]{:S(2)}) %collective-permute-start.1) | collective-permute-done | bytes 4194336 | tf_op jit(solution)/shard_map/ppermute | solution.py:128
  451.3 2.5 fusion.44
  453.8 6.1 %all-to-all-start.3 = ((bf16[32,16,512]{2,1,0:T(8,128)(2,1)}), bf16[32,16,512]{2,1,0:T(8,128)(2,1)S(1)}, u32[]{:S(2)}, u32[]{:S(2)}) async-start(bf16[32,16,512]{2,1,0:T(8,128)(2,1)} %bitcast.26), calls=%async_computation.3 | async-start | bytes 1048576 | tf_op jit(solution)/shard_map/all_to_all | solution.py:131
  459.9 3.8 copy.39
  463.7 3.8 copy.40
  467.6 3.8 copy.41
  (52 shorter events, 12.8 us)
Async XLA Ops:
  7.9 4.1 copy-start.10
  7.9 4.4 copy-start.12
  12.3 2.5 copy-start.8
  14.8 10.7 %copy-start.6 = (f32[1,1024]{1,0:T(1,128)S(1)}, f32[1,1024]{1,0:T(1,128)}, u32[]{:S(2)}) copy-start(f32[1,1024]{1,0:T(1,128)} %param.18) | copy-start | bytes 12292
  93.6 3.5 copy-start.9
  97.1 2.2 copy-start.11
  99.3 1.1 copy-start.14
  151.0 4.5 copy-start.13
  155.5 12.8 %copy-start.7 = (s32[32]{0:T(128)S(1)}, s32[32]{0:T(128)}, u32[]{:S(2)}) copy-start(s32[32]{0:T(128)} %param.21) | copy-start | bytes 388
  166.9 1.4 copy-start
  177.4 4.8 copy-start.5
  177.4 43.8 %all-to-all-start.2 = ((bf16[32,3,6,2048]{3,2,1,0:T(8,128)(2,1)}), bf16[32,3,6,2048]{3,2,1,0:T(8,128)(2,1)S(1)}, u32[]{:S(2)}, u32[]{:S(2)}) async-start(bf16[32,3,6,2048]{3,2,1,0:T(8,128)(2,1)} %copy.38), calls=%async_computation.2 | async-start | bytes 6291456 | tf_op jit(solution)/shard_map/all_to_all | solution.py:104
  181.4 23.6 %all-gather.2.cloned.1.call-start = ((), (), s32[]{:S(2)}) async-start(), calls=%async_computation.4 | async-start | bytes 1310720 | tf_op jit(solution)/shard_map/all_gather | solution.py:117
  221.2 33.7 %all-to-all-start = ((bf16[32,16,2048]{2,1,0:T(8,128)(2,1)}), bf16[32,16,2048]{2,1,0:T(8,128)(2,1)}, u32[]{:S(2)}, u32[]{:S(2)}) async-start(bf16[32,16,2048]{2,1,0:T(8,128)(2,1)} %bitcast.132), calls=%async_computation | async-start | bytes 4194304 | tf_op jit(solution)/shard_map/all_to_all | solution.py:122
  228.2 2.9 copy-start.2
  262.6 91.5 %collective-permute-start = (f32[512,2048]{1,0:T(8,128)}, f32[512,2048]{1,0:T(8,128)S(1)}, u32[]{:S(2)}, u32[]{:S(2)}) collective-permute-start(f32[512,2048]{1,0:T(8,128)} %fusion.43), channel_id=1, source_target_pairs={{0,1},{1,0},{2,3},{3,2},{4,5},{5,4},{6,7},{7,6},{8,9},{9,8},{10,11... | collective-permute-start | bytes 12582920 | tf_op jit(solution)/shard_map/ppermute | solution.py:128
  359.0 100.9 %copy-start.1 = (f32[16,3,1,12288]{3,0,1,2:T(8,128)S(1)}, f32[16,3,1,12288]{3,0,1,2:T(8,128)}, u32[]{:S(2)}) copy-start(f32[16,3,1,12288]{3,0,1,2:T(8,128)} %copy-done) | copy-start | bytes 7077892
  359.0 92.3 %collective-permute-start.1 = (f32[512,2048]{1,0:T(8,128)}, f32[512,2048]{1,0:T(8,128)}, u32[]{:S(2)}, u32[]{:S(2)}) collective-permute-start(f32[512,2048]{1,0:T(8,128)} %add.58), channel_id=1, source_target_pairs={{0,2},{1,3},{2,0},{3,1},{4,6},{5,7},{6,4},{7,5},{8,10},{9,11},{10,... | collective-permute-start | bytes 12582920 | tf_op jit(solution)/shard_map/ppermute | solution.py:128
  453.8 17.8 %all-to-all-start.3 = ((bf16[32,16,512]{2,1,0:T(8,128)(2,1)}), bf16[32,16,512]{2,1,0:T(8,128)(2,1)S(1)}, u32[]{:S(2)}, u32[]{:S(2)}) async-start(bf16[32,16,512]{2,1,0:T(8,128)(2,1)} %bitcast.26), calls=%async_computation.3 | async-start | bytes 1048576 | tf_op jit(solution)/shard_map/all_to_all | solution.py:131
  459.9 3.8 copy-start.4
  463.7 3.8 copy-start.3
Sparse Core Ops, SparseCore 0:
  183.9 21.0 all-gather.1
